TPU v7x, 32 devices: a whole 2x2x4 slice. The times are simulated.
32 devices in a mesh: freq: 4 (over y, core), space: 8 (over z, x).
Axes of the slice: x: 2, y: 2, z: 4, core: 2. Of those that a mesh axis runs over, the one named last changes fastest.
Arguments:
- traces: float32 [1024, 512, 256], P(('freq', 'space')), may hold values from -50 to 50
- probes: float32 [8, 128, 64], P('freq'), may hold values from -0.5 to 0.5
Outputs:
- denoised: float32 [1024, 512, 256], P(('freq', 'space'))
All inputs are finite; a program needn't handle non-finite values.
Results may differ from a plain program's by a relative error of at most 0.000092.
Values sent between devices are 32-bit elements; how exact they have to be, the bound alone decides.
No kernel may reach another device: no remote copies, remote signals or barrier semaphores. Data moves between devices by JAX's collectives and lax.ppermute only.
A program may use at most 192 MiB of HBM per device.

v0:
```python
import jax
import jax.numpy as jnp
from jax import lax
from jax.sharding import PartitionSpec as P

NT = 1024
BAND_LO = 16
HIGHEST_PRECISION = lax.Precision.HIGHEST


def wave_table(freq_ids, time_ids, period, factor):
    phase = (freq_ids[:, None] * time_ids[None, :] % period).astype(jnp.float32) * (
        2.0 * jnp.pi / period
    )
    return jnp.stack([jnp.cos(phase), -jnp.sin(phase)]) * factor


def hankel(spectrum, window, columns):
    width = spectrum.shape[-1]
    tiled = jnp.tile(spectrum, (1, 1, window + 1))[:, :, : window * (width + 1)]
    return tiled.reshape(spectrum.shape[0], spectrum.shape[1], window, width + 1)[:, :, :, :columns]


def diag_mean(blocks, width):
    halves, channels, window, columns = blocks.shape
    padded = jnp.pad(blocks, ((0, 0), (0, 0), (0, 0), (0, width + 1 - columns)))
    flat_rows = padded.reshape(halves, channels, window * (width + 1))
    flat_rows = jnp.pad(flat_rows, ((0, 0), (0, 0), (0, width - window)))
    totals = flat_rows.reshape(halves, channels, window + 1, width).sum(axis=2)
    position = jnp.arange(width, dtype=jnp.int32)
    counts = jnp.minimum(jnp.minimum(position + 1, width - position), min(window, columns))
    return totals / counts.astype(jnp.float32)


def assemble(gram_raw, cross_raw):
    half = gram_raw.shape[-1] // 2
    diagonal_part = gram_raw[..., :half, :half] + gram_raw[..., half:, half:]
    skew_part = gram_raw[..., half:, :half] - gram_raw[..., :half, half:]
    gram_matrix = jnp.concatenate(
        [
            jnp.concatenate([diagonal_part, skew_part], -1),
            jnp.concatenate([-skew_part, diagonal_part], -1),
        ],
        -2,
    )
    real_rows = cross_raw[..., 0, :, :]
    imag_rows = cross_raw[..., 1, :, :]
    cross_terms = jnp.concatenate(
        [
            real_rows[..., :half, :] + imag_rows[..., half:, :],
            imag_rows[..., :half, :] - real_rows[..., half:, :],
        ],
        -2,
    )
    return (gram_matrix, cross_terms)


def solve_one(factor_rows, right_rows):
    return jax.scipy.linalg.cho_solve((factor_rows, True), right_rows)


def first_pass(slice_pair):
    spectrum, probe = slice_pair
    width = spectrum.shape[-1]
    window = width // 2 + 1
    columns = width // 2
    channels = spectrum.shape[1]
    hankel_rows = hankel(spectrum, window, columns).reshape(2, channels * window, columns)
    sketch_basis = jnp.einsum(
        "qrp,pk->rqk", hankel_rows, probe, precision=HIGHEST_PRECISION
    ).reshape(channels * window, 2 * probe.shape[1])
    gram_raw = jnp.dot(sketch_basis.T, sketch_basis, precision=HIGHEST_PRECISION)
    cross_raw = jnp.einsum("rk,qrp->qkp", sketch_basis, hankel_rows, precision=HIGHEST_PRECISION)
    return (sketch_basis, gram_raw, cross_raw)


def body(traces, probes):
    time_slab = lax.all_to_all(traces, "space", split_axis=1, concat_axis=0, tiled=True)
    time_local = time_slab.shape[0]
    channels = time_slab.shape[1]
    width = time_slab.shape[2]
    freq_local = probes.shape[0]
    freq_total = freq_local * lax.axis_size("freq")
    time_ids = lax.axis_index("freq") * time_local + jnp.arange(time_local, dtype=jnp.int32)
    freq_ids = (
        BAND_LO + jnp.int32(0) + jnp.arange(lax.axis_size("freq") * freq_local, dtype=jnp.int32)
    )
    wave_rows = wave_table(freq_ids, time_ids, NT, NT ** (-0.5))
    spectra = lax.psum_scatter(
        jnp.einsum("qft,tcx->fqcx", wave_rows, time_slab, precision=HIGHEST_PRECISION),
        "freq",
        scatter_dimension=0,
        tiled=True,
    )
    sketch_basis, gram_raw, cross_raw = lax.map(first_pass, (spectra, probes))
    gram_sum, cross_sum = lax.psum((gram_raw, cross_raw), "space")
    gram_matrix, cross_terms = assemble(gram_sum, cross_sum)
    lower_factor = jnp.linalg.cholesky(gram_matrix)
    coeffs = jax.vmap(solve_one)(lower_factor, cross_terms)
    window = width // 2 + 1
    columns = width // 2

    def second_pass(slice_pair):
        basis_rows, coeff_rows = slice_pair
        half = coeff_rows.shape[0] // 2
        real_part = coeff_rows[:half]
        imag_part = coeff_rows[half:]
        mixing = jnp.stack(
            [
                jnp.concatenate([real_part, -imag_part], 0),
                jnp.concatenate([imag_part, real_part], 0),
            ]
        )
        rebuilt = jnp.einsum("rk,qkp->qrp", basis_rows, mixing, precision=HIGHEST_PRECISION)
        return diag_mean(rebuilt.reshape(2, channels, window, columns), width)

    clean = lax.map(second_pass, (sketch_basis, coeffs))
    start_volume = jnp.zeros((time_local, channels, width), jnp.float32)
    shard_piece = lax.all_gather(clean, "freq", axis=0, tiled=True)
    freq_ids = BAND_LO + jnp.int32(0) + jnp.arange(shard_piece.shape[0], dtype=jnp.int32)
    wave_rows = wave_table(freq_ids, time_ids, NT, (2.0 / freq_total) ** 0.5)
    volume = start_volume + jnp.einsum(
        "qft,fqcx->tcx", wave_rows, shard_piece, precision=HIGHEST_PRECISION
    )
    return lax.all_to_all(volume, "space", split_axis=0, concat_axis=1, tiled=True)


def solution(mesh):
    in_specs = (P(("freq", "space"), None, None), P("freq", None, None))
    out_specs = P(("freq", "space"), None, None)
    return jax.shard_map(body, mesh=mesh, in_specs=in_specs, out_specs=out_specs, check_vma=False)
```

profile of v0, /device:TPU:0, one launch (start us, length us, event | category | flops | bytes accessed | tf_op | source)
XLA Modules:
  0.0 1406.5 jit_solution(224654636673980314)
XLA Ops:
  6.5 17.8 %copy.34 = f32[32,512,256]{2,0,1:T(8,128)} copy(f32[32,512,256]{2,1,0:T(8,128)} %param.6) | data formatting | bytes 33554432 | tf_op args[0]
  32.2 362.5 %all-to-all-done = f32[32,512,256]{2,0,1:T(8,128)} async-done(((f32[32,512,256]{2,0,1:T(8,128)}), f32[32,512,256]{2,0,1:T(8,128)}, u32[]{:S(2)}, u32[]{:S(2)}) %all-to-all-start) | async-done | bytes 16777248 | tf_op jit(solution)/shard_map/all_to_all | solution.py:78
  410.7 23.8 %reduce-scatter.2.cloned.1.call-done = f32[2,2,64,256]{3,2,1,0:T(8,128)} async-done(((f32[8,2,64,256]{3,2,1,0:T(8,128)}), f32[2,2,64,256]{3,2,1,0:T(8,128)}) %reduce-scatter.2.cloned.1.call-update) | async-done | bytes 262160 | tf_op jit(solution)/shard_map/reduce_scatter | solution.py:89
  434.6 237.5 %while.26 = (s32[]{:T(128)}, f32[2,8256,128]{2,1,0:T(8,128)}, f32[2,128,128]{1,2,0:T(8,128)S(1)}, f32[2,2,128,128]{3,2,0,1:T(8,128)S(1)}, f32[2,128,64]{1,2,0:T(...) while((s32[]{:T(128)}, f32[2,8256,128]{2,1,0:T(8,128)}, f32[2,128,128]{1,2,0:T(8,128)S(1)}, ...), condition=%wide.region_2.3_spmd, body=%wide.region_1.2_spmd.sunk | while | flops 6492782592 | bytes 234325712 | solution.py:95
  459.7 18.4 %tile.14 = f32[2,64,33280]{2,1,0:T(8,128)} reshape(f32[2,64,130,256]{3,2,1,0:T(8,128)} %tile.13) | data formatting | bytes 34078720 | tf_op jit(solution)/shard_map/while/body/eval_jaxpr/tile | solution.py:20
  478.1 23.7 %reshape.225 = f32[2,64,129,257]{3,2,1,0:T(8,128)} reshape(f32[2,64,33153]{2,1,0:T(8,128)} %bitcast.128) | data formatting | bytes 33948672 | tf_op jit(solution)/shard_map/while/body/eval_jaxpr/reshape | solution.py:21
  532.8 13.7 convolution_bitcast_fusion.7
  569.9 18.4 %tile.14 = f32[2,64,33280]{2,1,0:T(8,128)} reshape(f32[2,64,130,256]{3,2,1,0:T(8,128)} %tile.13) | data formatting | bytes 34078720 | tf_op jit(solution)/shard_map/while/body/eval_jaxpr/tile | solution.py:20
  588.3 23.7 %reshape.225 = f32[2,64,129,257]{3,2,1,0:T(8,128)} reshape(f32[2,64,33153]{2,1,0:T(8,128)} %bitcast.128) | data formatting | bytes 33948672 | tf_op jit(solution)/shard_map/while/body/eval_jaxpr/reshape | solution.py:21
  643.0 13.7 convolution_bitcast_fusion.7
  672.9 72.1 %all-reduce.5.cloned.1.call-done = (f32[2,2,128,128]{3,2,0,1:T(8,128)}, f32[2,128,128]{1,2,0:T(8,128)}) async-done(((f32[2,2,128,128]{3,2,0,1:T(8,128)}, f32[2,128,128]{1,2,0:T(8,128)}), (f32[2,2,128,128]{3,2,0,1:T(8,128)}, f32[2,128,128]{1,2,0:T(8,128)})) %all-reduce.5.cloned.1.call-update) | async-done | bytes 393232 | tf_op jit(solution)/shard_map/psum | solution.py:96
  746.4 23.5 %custom-call.11 = f32[2,128,128]{2,1,0:T(8,128)S(1)} custom-call(f32[2,128,128]{2,1,0:T(8,128)S(1)} %fusion.24), custom_call_target="Cholesky" | custom-call | tf_op jit(solution)/shard_map/jit(cholesky)/cholesky | solution.py:98
  770.1 19.7 %custom-call.12 = f32[2,1,128,128]{2,3,1,0:T(8,128)S(1)} custom-call(f32[2,1,128,128]{3,2,1,0:T(8,128)S(1)} %select_bitcast_fusion), custom_call_target="InvertDiagBlocksLowerTriangular" | custom-call | tf_op jit(solution)/shard_map/vmap(jit(_cho_solve))/triangular_solve | solution.py:59
  791.5 184.5 %while.27 = (s32[]{:T(128)}, f32[2,2,64,256]{3,2,1,0:T(8,128)S(1)}, f32[2,128,128]{2,1,0:T(8,128)S(1)}, f32[2,8256,128]{2,1,0:T(8,128)}, s32[]{:T(128)}, /*index=5*/s32[]{:T(128)}, s32[]{}, f32[]{:T(128)}) while((s32[]{:T(128)}, f32[2,2,64,256]{3,2,1,0:T(8,128)S(1)}, f32[2,128,128]{2,1,0:T(8,128)S(1)}, f32[2,8256,128]{2,1,0:T(8,128)}, ...), condition=%wide.region_9.10_spmd, body=%wide.region_7.9_spmd.sunk | while | flops 3250726144 | bytes 175018624 | solution.py:117
  811.3 12.3 pad.84
  823.6 22.5 %reshape.228 = f32[2,64,33153]{2,1,0:T(8,128)} reshape(f32[2,64,129,257]{3,2,1,0:T(8,128)} %pad.84) | data formatting | bytes 33948672 | tf_op jit(solution)/shard_map/while/body/eval_jaxpr/reshape | solution.py:27
  857.5 18.3 %reshape.229 = f32[2,64,130,256]{3,2,1,0:T(8,128)} reshape(f32[2,64,33280]{2,1,0:T(8,128)} %pad.85) | data formatting | bytes 34078720 | tf_op jit(solution)/shard_map/while/body/eval_jaxpr/reshape | solution.py:29
  903.5 12.3 pad.84
  915.7 22.5 %reshape.228 = f32[2,64,33153]{2,1,0:T(8,128)} reshape(f32[2,64,129,257]{3,2,1,0:T(8,128)} %pad.84) | data formatting | bytes 33948672 | tf_op jit(solution)/shard_map/while/body/eval_jaxpr/reshape | solution.py:27
  949.6 18.3 %reshape.229 = f32[2,64,130,256]{3,2,1,0:T(8,128)} reshape(f32[2,64,33280]{2,1,0:T(8,128)} %pad.85) | data formatting | bytes 34078720 | tf_op jit(solution)/shard_map/while/body/eval_jaxpr/reshape | solution.py:29
  976.8 15.9 %all-gather.2.cloned.1.call-done = f32[8,2,64,256]{3,2,1,0:T(8,128)} async-done(((f32[2,2,64,256]{3,2,1,0:T(8,128)}), f32[8,2,64,256]{3,2,1,0:T(8,128)}) %all-gather.2.cloned.1.call-update) | async-done | bytes 1048592 | tf_op jit(solution)/shard_map/all_gather | solution.py:119
  992.7 14.8 %convolution_bitcast_fusion.3 = f32[256,64,256]{2,0,1:T(8,128)S(1)} fusion(f32[8,2,64,256]{3,2,1,0:T(8,128)} %all-gather.2.cloned.1.call-done, f32[1,8,256]{2,1,0:T(8,128)S(1)} %copy-done.9, f32[1,8,256]{2,1,0:T(8,128)S(1)} %copy-done.7), kind=kOutput, calls=%fused_computation.29 | convolution fusion | flops 805314560 | bytes 17842176 | tf_op jit(solution)/shard_map/qft,fqcx->tcx/dot_general | solution.py:122
  1007.5 17.6 %copy.43 = f32[256,64,256]{2,1,0:T(8,128)S(1)} copy(f32[256,64,256]{2,0,1:T(8,128)S(1)} %convolution_bitcast_fusion.3) | data formatting | bytes 33554432 | tf_op jit(solution)/shard_map/qft,fqcx->tcx/dot_general | solution.py:122
  1025.1 368.5 %all_to_all.36 = f32[256,64,256]{2,1,0:T(8,128)S(1)} all-to-all(f32[256,64,256]{2,1,0:T(8,128)S(1)} %copy.43), channel_id=1, replica_groups=mesh['freq'=4,'space'=8] {'space'}, dimensions={0} | all-to-all | bytes 33554432 | tf_op jit(solution)/shard_map/all_to_all | solution.py:125
  (103 shorter events, 221.7 us)
Async XLA Ops:
  24.3 370.4 %all-to-all-start = ((f32[32,512,256]{2,0,1:T(8,128)}), f32[32,512,256]{2,0,1:T(8,128)}, u32[]{:S(2)}, u32[]{:S(2)}) async-start(f32[32,512,256]{2,0,1:T(8,128)} %copy.34), calls=%async_computation | async-start | bytes 33554432 | tf_op jit(solution)/shard_map/all_to_all | solution.py:78
  31.6 403.0 %reduce-scatter.2.cloned.1.call-start = ((), (), s32[]{:S(2)}) async-start(), calls=%async_computation.3 | async-start | bytes 1310720 | tf_op jit(solution)/shard_map/reduce_scatter | solution.py:89
  32.2 369.1 %copy-start.6 = (f32[1,8,256]{2,1,0:T(8,128)}, f32[1,8,256]{2,1,0:T(8,128)S(1)}, u32[]{:S(2)}) copy-start(f32[1,8,256]{2,1,0:T(8,128)S(1)} %get-tuple-element.157) | copy-start | bytes 24580
  32.2 369.1 %copy-start.8 = (f32[1,8,256]{2,1,0:T(8,128)}, f32[1,8,256]{2,1,0:T(8,128)S(1)}, u32[]{:S(2)}) copy-start(f32[1,8,256]{2,1,0:T(8,128)S(1)} %get-tuple-element.158) | copy-start | bytes 24580
  401.3 33.2 %copy-start.2 = (f32[2,128,64]{1,2,0:T(8,128)S(1)}, f32[2,128,64]{1,2,0:T(8,128)}, u32[]{:S(2)}) copy-start(f32[2,128,64]{1,2,0:T(8,128)} %param.7) | copy-start | bytes 196612
  410.6 334.4 %all-reduce.5.cloned.1.call-start = ((), (), s32[]{:S(2)}) async-start(), calls=%async_computation.5 | async-start | bytes 786432 | tf_op jit(solution)/shard_map/psum | solution.py:96
  518.8 14.0 copy-start.1
  530.7 2.0 copy-start
  552.3 5.0 slice-start
  552.3 5.0 slice-start.1
  629.0 14.0 copy-start.1
  640.9 2.0 copy-start
  662.5 5.0 slice-start
  662.5 5.0 slice-start.1
  672.1 0.7 copy-start.3
  672.1 0.7 copy-start.5
  672.8 319.8 %all-gather.2.cloned.1.call-start = ((), (), s32[]{:S(2)}) async-start(), calls=%async_computation.4 | async-start | bytes 1310720 | tf_op jit(solution)/shard_map/all_gather | solution.py:119
  791.5 201.1 %copy-start.7 = (f32[1,8,256]{2,1,0:T(8,128)S(1)}, f32[1,8,256]{2,1,0:T(8,128)}, u32[]{:S(2)}) copy-start(f32[1,8,256]{2,1,0:T(8,128)} %copy-done.6) | copy-start | bytes 24580
  791.5 201.1 %copy-start.9 = (f32[1,8,256]{2,1,0:T(8,128)S(1)}, f32[1,8,256]{2,1,0:T(8,128)}, u32[]{:S(2)}) copy-start(f32[1,8,256]{2,1,0:T(8,128)} %copy-done.8) | copy-start | bytes 24580
  976.1 0.7 copy-start.4
Sparse Core Ops, SparseCore 0:
  410.8 23.7 reduce-scatter.1
  673.0 72.0 all-reduce.4
  976.9 15.7 all-gather.1
where the time goes:
time: 1420 us; the launch traced here: 1410 us
  waiting for transfers between devices  474 us (33%)
  blocking collectives  368 us (26%)
  local copies, waits for them, and re-layouts  360 us (25%)
  matrix products  104 us (7%)
  other arithmetic  61 us (4%)
  loops' own time  17.5 us (1%)
    all_to_all x1, blocking collectives, body(): lax.all_to_all(volume, 'space', split_axis=0, concat_axis=1, tiled=True)  368 us
    all_to_all x1, waiting for transfers between devices, body(): lax.all_to_all(traces, 'space', split_axis=1, concat_axis=0, tiled=True)  362 us
    psum x1, waiting for transfers between devices, body(): gram_sum, cross_sum = lax.psum((gram_raw, cross_raw), 'space')  72.1 us
    another operation x6, local copies, waits for them, and re-layouts, hankel(): tiled = jnp.tile(spectrum, (1, 1, window + 1))[:, :, :window * (width + 1)]  53.7 us
    reshape x2, local copies, waits for them, and re-layouts, hankel(): tiled.reshape(spectrum.shape[0], spectrum.shape[1], window, width + 1)  47.4 us
    reshape x2, local copies, waits for them, and re-layouts, diag_mean(): flat_rows = padded.reshape(halves, channels, window * (width + 1))  44.9 us
    reshape x2, local copies, waits for them, and re-layouts, diag_mean(): totals = flat_rows.reshape(halves, channels, window + 1, width).sum(axis=2)  36.6 us
  transfers between devices with their start and end apart: 4, of which 4 were waited for; matrix products, arithmetic and copies ran while one was open for 0% of the time, Pallas kernels for 0%

commit v1 on v0

--- a/solution.py
+++ b/solution.py
@@ -122,7 +122,10 @@
     volume = start_volume + jnp.einsum(
         "qft,fqcx->tcx", wave_rows, shard_piece, precision=HIGHEST_PRECISION
     )
-    return lax.all_to_all(volume, "space", split_axis=0, concat_axis=1, tiled=True)
+    return jnp.concatenate(
+        lax.all_to_all(jnp.stack(jnp.split(volume, lax.axis_size("space"), axis=0)), "space", 0, 0),
+        axis=1,
+    )
 
 
 def solution(mesh):

time: 1420 us -> 1420 us (level)
    reshape x0 -> x1, local copies, waits for them, and re-layouts: none -> 19.3 us  [body(): jnp.concatenate(lax.all_to_all(jnp.stack(jnp.split(volume, lax.axis_size(...]
    dot_general x1 -> x0, local copies, waits for them, and re-layouts: 17.6 us -> none  [body(): jnp.einsum('qft,fqcx->tcx', wave_rows, shard_piece, precision=HIGHEST_PRE...]
where the time goes in v1:
time: 1420 us; the launch traced here: 1410 us
  waiting for transfers between devices  474 us (33%)
  blocking collectives  369 us (26%)
  local copies, waits for them, and re-layouts  353 us (25%)
  matrix products  111 us (8%)
  other arithmetic  61 us (4%)
  loops' own time  17.5 us (1%)
    all_to_all x1, blocking collectives, body(): lax.all_to_all(jnp.stack(jnp.split(volume, lax.axis_size('space'), axis=0...  369 us
    all_to_all x1, waiting for transfers between devices, body(): lax.all_to_all(traces, 'space', split_axis=1, concat_axis=0, tiled=True)  362 us
    psum x1, waiting for transfers between devices, body(): gram_sum, cross_sum = lax.psum((gram_raw, cross_raw), 'space')  72.1 us
    another operation x6, local copies, waits for them, and re-layouts, hankel(): tiled = jnp.tile(spectrum, (1, 1, window + 1))[:, :, :window * (width + 1)]  53.7 us
    reshape x2, local copies, waits for them, and re-layouts, hankel(): tiled.reshape(spectrum.shape[0], spectrum.shape[1], window, width + 1)  47.3 us
    reshape x2, local copies, waits for them, and re-layouts, diag_mean(): flat_rows = padded.reshape(halves, channels, window * (width + 1))  44.9 us
    reshape x2, local copies, waits for them, and re-layouts, diag_mean(): totals = flat_rows.reshape(halves, channels, window + 1, width).sum(axis=2)  36.6 us
  transfers between devices with their start and end apart: 4, of which 4 were waited for; matrix products, arithmetic and copies ran while one was open for 0% of the time, Pallas kernels for 0%

profile of v1, /device:TPU:0, one launch (start us, length us, event | category | flops | bytes accessed | tf_op | source)
XLA Modules:
  0.0 1407.6 jit_solution(4780748302705515981)
XLA Ops:
  6.5 17.8 %copy.33 = f32[32,512,256]{2,0,1:T(8,128)} copy(f32[32,512,256]{2,1,0:T(8,128)} %param.6) | data formatting | bytes 33554432 | tf_op args[0]
  32.3 362.4 %all-to-all-done = f32[32,512,256]{2,0,1:T(8,128)} async-done(((f32[32,512,256]{2,0,1:T(8,128)}), f32[32,512,256]{2,0,1:T(8,128)}, u32[]{:S(2)}, u32[]{:S(2)}) %all-to-all-start) | async-done | bytes 16777248 | tf_op jit(solution)/shard_map/all_to_all | solution.py:78
  410.7 23.9 %reduce-scatter.2.cloned.1.call-done = f32[2,2,64,256]{3,2,1,0:T(8,128)} async-done(((f32[8,2,64,256]{3,2,1,0:T(8,128)}), f32[2,2,64,256]{3,2,1,0:T(8,128)}) %reduce-scatter.2.cloned.1.call-update) | async-done | bytes 262160 | tf_op jit(solution)/shard_map/reduce_scatter | solution.py:89
  434.6 241.6 %while.26 = (s32[]{:T(128)}, f32[2,8256,128]{2,1,0:T(8,128)}, f32[2,128,128]{1,2,0:T(8,128)S(1)}, f32[2,2,128,128]{3,2,0,1:T(8,128)S(1)}, f32[2,128,64]{1,2,0:T(...) while((s32[]{:T(128)}, f32[2,8256,128]{2,1,0:T(8,128)}, f32[2,128,128]{1,2,0:T(8,128)S(1)}, ...), condition=%wide.region_2.3_spmd, body=%wide.region_1.2_spmd.sunk | while | flops 6492782592 | bytes 221546640 | solution.py:95
  459.8 18.4 %tile.14 = f32[2,64,33280]{2,1,0:T(8,128)} reshape(f32[2,64,130,256]{3,2,1,0:T(8,128)} %tile.13) | data formatting | bytes 34078720 | tf_op jit(solution)/shard_map/while/body/eval_jaxpr/tile | solution.py:20
  478.1 23.6 %reshape.233 = f32[2,64,129,257]{3,2,1,0:T(8,128)} reshape(f32[2,64,33153]{2,1,0:T(8,128)} %bitcast.157) | data formatting | bytes 33948672 | tf_op jit(solution)/shard_map/while/body/eval_jaxpr/reshape | solution.py:21
  532.6 13.7 convolution_bitcast_fusion.7
  572.0 18.4 %tile.14 = f32[2,64,33280]{2,1,0:T(8,128)} reshape(f32[2,64,130,256]{3,2,1,0:T(8,128)} %tile.13) | data formatting | bytes 34078720 | tf_op jit(solution)/shard_map/while/body/eval_jaxpr/tile | solution.py:20
  590.4 23.6 %reshape.233 = f32[2,64,129,257]{3,2,1,0:T(8,128)} reshape(f32[2,64,33153]{2,1,0:T(8,128)} %bitcast.157) | data formatting | bytes 33948672 | tf_op jit(solution)/shard_map/while/body/eval_jaxpr/reshape | solution.py:21
  644.8 13.7 convolution_bitcast_fusion.7
  677.1 72.1 %all-reduce.5.cloned.1.call-done = (f32[2,2,128,128]{3,2,0,1:T(8,128)}, f32[2,128,128]{1,2,0:T(8,128)}) async-done(((f32[2,2,128,128]{3,2,0,1:T(8,128)}, f32[2,128,128]{1,2,0:T(8,128)}), (f32[2,2,128,128]{3,2,0,1:T(8,128)}, f32[2,128,128]{1,2,0:T(8,128)})) %all-reduce.5.cloned.1.call-update) | async-done | bytes 393232 | tf_op jit(solution)/shard_map/psum | solution.py:96
  750.6 23.5 %custom-call.11 = f32[2,128,128]{2,1,0:T(8,128)S(1)} custom-call(f32[2,128,128]{2,1,0:T(8,128)S(1)} %fusion.32), custom_call_target="Cholesky" | custom-call | tf_op jit(solution)/shard_map/jit(cholesky)/cholesky | solution.py:98
  774.3 19.7 %custom-call.12 = f32[2,1,128,128]{2,3,1,0:T(8,128)S(1)} custom-call(f32[2,1,128,128]{3,2,1,0:T(8,128)S(1)} %select_bitcast_fusion), custom_call_target="InvertDiagBlocksLowerTriangular" | custom-call | tf_op jit(solution)/shard_map/vmap(jit(_cho_solve))/triangular_solve | solution.py:59
  795.7 184.5 %while.27 = (s32[]{:T(128)}, f32[2,2,64,256]{3,2,1,0:T(8,128)S(1)}, f32[2,128,128]{2,1,0:T(8,128)S(1)}, f32[2,8256,128]{2,1,0:T(8,128)}, s32[]{:T(128)}, /*index=5*/s32[]{:T(128)}, s32[]{}, f32[]{:T(128)}) while((s32[]{:T(128)}, f32[2,2,64,256]{3,2,1,0:T(8,128)S(1)}, f32[2,128,128]{2,1,0:T(8,128)S(1)}, f32[2,8256,128]{2,1,0:T(8,128)}, ...), condition=%wide.region_9.10_spmd, body=%wide.region_7.9_spmd.sunk | while | flops 3250726144 | bytes 175018624 | solution.py:117
  815.4 12.3 pad.84
  827.7 22.5 %reshape.236 = f32[2,64,33153]{2,1,0:T(8,128)} reshape(f32[2,64,129,257]{3,2,1,0:T(8,128)} %pad.84) | data formatting | bytes 33948672 | tf_op jit(solution)/shard_map/while/body/eval_jaxpr/reshape | solution.py:27
  861.6 18.3 %reshape.237 = f32[2,64,130,256]{3,2,1,0:T(8,128)} reshape(f32[2,64,33280]{2,1,0:T(8,128)} %pad.85) | data formatting | bytes 34078720 | tf_op jit(solution)/shard_map/while/body/eval_jaxpr/reshape | solution.py:29
  907.6 12.3 pad.84
  919.9 22.5 %reshape.236 = f32[2,64,33153]{2,1,0:T(8,128)} reshape(f32[2,64,129,257]{3,2,1,0:T(8,128)} %pad.84) | data formatting | bytes 33948672 | tf_op jit(solution)/shard_map/while/body/eval_jaxpr/reshape | solution.py:27
  953.8 18.3 %reshape.237 = f32[2,64,130,256]{3,2,1,0:T(8,128)} reshape(f32[2,64,33280]{2,1,0:T(8,128)} %pad.85) | data formatting | bytes 34078720 | tf_op jit(solution)/shard_map/while/body/eval_jaxpr/reshape | solution.py:29
  980.9 15.9 %all-gather.2.cloned.1.call-done = f32[8,2,64,256]{3,2,1,0:T(8,128)} async-done(((f32[2,2,64,256]{3,2,1,0:T(8,128)}), f32[8,2,64,256]{3,2,1,0:T(8,128)}) %all-gather.2.cloned.1.call-update) | async-done | bytes 1048592 | tf_op jit(solution)/shard_map/all_gather | solution.py:119
  996.8 14.8 %convolution_bitcast_fusion.3 = f32[256,64,256]{2,0,1:T(8,128)S(1)} fusion(f32[8,2,64,256]{3,2,1,0:T(8,128)} %all-gather.2.cloned.1.call-done, f32[1,8,256]{2,1,0:T(8,128)S(1)} %copy-done.9, f32[1,8,256]{2,1,0:T(8,128)S(1)} %copy-done.7), kind=kOutput, calls=%fused_computation.29 | convolution fusion | flops 805314560 | bytes 17842176 | tf_op jit(solution)/shard_map/qft,fqcx->tcx/dot_general | solution.py:122
  1012.8 368.7 %all_to_all.23 = f32[8,32,64,256]{3,1,2,0:T(8,128)S(1)} all-to-all(f32[8,32,64,256]{3,1,2,0:T(8,128)S(1)} %fusion.16), channel_id=1, replica_groups=mesh['freq'=4,'space'=8] {'space'}, dimensions={0} | all-to-all | bytes 33554432 | tf_op jit(solution)/shard_map/all_to_all | solution.py:126
  1381.5 19.3 %copy.42 = f32[32,512,256]{2,1,0:T(8,128)} copy(f32[32,512,256]{2,0,1:T(8,128)S(1)} %bitcast.159) | data formatting | bytes 33554432 | tf_op jit(solution)/shard_map/reshape | solution.py:125
  (100 shorter events, 220.9 us)
Async XLA Ops:
  24.3 370.4 %all-to-all-start = ((f32[32,512,256]{2,0,1:T(8,128)}), f32[32,512,256]{2,0,1:T(8,128)}, u32[]{:S(2)}, u32[]{:S(2)}) async-start(f32[32,512,256]{2,0,1:T(8,128)} %copy.33), calls=%async_computation | async-start | bytes 33554432 | tf_op jit(solution)/shard_map/all_to_all | solution.py:78
  31.6 403.0 %reduce-scatter.2.cloned.1.call-start = ((), (), s32[]{:S(2)}) async-start(), calls=%async_computation.3 | async-start | bytes 1310720 | tf_op jit(solution)/shard_map/reduce_scatter | solution.py:89
  32.3 369.0 %copy-start.6 = (f32[1,8,256]{2,1,0:T(8,128)}, f32[1,8,256]{2,1,0:T(8,128)S(1)}, u32[]{:S(2)}) copy-start(f32[1,8,256]{2,1,0:T(8,128)S(1)} %get-tuple-element.157) | copy-start | bytes 24580
  32.3 369.0 %copy-start.8 = (f32[1,8,256]{2,1,0:T(8,128)}, f32[1,8,256]{2,1,0:T(8,128)S(1)}, u32[]{:S(2)}) copy-start(f32[1,8,256]{2,1,0:T(8,128)S(1)} %get-tuple-element.158) | copy-start | bytes 24580
  401.3 33.3 %copy-start.2 = (f32[2,128,64]{1,2,0:T(8,128)S(1)}, f32[2,128,64]{1,2,0:T(8,128)}, u32[]{:S(2)}) copy-start(f32[2,128,64]{1,2,0:T(8,128)} %param.7) | copy-start | bytes 196612
  410.6 338.6 %all-reduce.5.cloned.1.call-start = ((), (), s32[]{:S(2)}) async-start(), calls=%async_computation.5 | async-start | bytes 786432 | tf_op jit(solution)/shard_map/psum | solution.py:96
  518.6 14.0 copy-start.1
  530.6 2.0 copy-start
  630.9 14.0 copy-start.1
  642.8 2.0 copy-start
  676.2 0.7 copy-start.3
  676.2 0.7 copy-start.5
  677.0 319.8 %all-gather.2.cloned.1.call-start = ((), (), s32[]{:S(2)}) async-start(), calls=%async_computation.4 | async-start | bytes 1310720 | tf_op jit(solution)/shard_map/all_gather | solution.py:119
  795.6 201.2 %copy-start.7 = (f32[1,8,256]{2,1,0:T(8,128)S(1)}, f32[1,8,256]{2,1,0:T(8,128)}, u32[]{:S(2)}) copy-start(f32[1,8,256]{2,1,0:T(8,128)} %copy-done.6) | copy-start | bytes 24580
  795.7 201.2 %copy-start.9 = (f32[1,8,256]{2,1,0:T(8,128)S(1)}, f32[1,8,256]{2,1,0:T(8,128)}, u32[]{:S(2)}) copy-start(f32[1,8,256]{2,1,0:T(8,128)} %copy-done.8) | copy-start | bytes 24580
  980.2 0.7 copy-start.4
Sparse Core Ops, SparseCore 0:
  410.8 23.7 reduce-scatter.1
  677.1 72.0 all-reduce.4
  981.0 15.7 all-gather.1
